TPU v7x, 256 devices: a whole 4x4x8 slice. The times are simulated.
256 devices in a mesh: seq: 32 (over z, x_hi, core), tp: 8 (over x_lo, y).
Axes of the slice: x: 4 (x_hi: 2, x_lo: 2; x = x_hi * 2 + x_lo), y: 4, z: 8, core: 2. Of those that a mesh axis runs over, the one named last changes fastest.
Arguments:
- tokens: bfloat16 [8192, 2048], P('seq', 'tp'), may hold values from -6 to 6
- ctx_len: int32 [32], P('seq'), may hold values from 0 to 12288, as said below
- cache_kv: bfloat16 [32, 4096, 2, 2048], P('seq', None, None, 'tp'), may hold values from -80 to 80, as said below
- cache_pos: int32 [32, 4096], P('seq'), may hold values from -1 to 12287, as said below
- attn_gain: float32 [2048], replicated, may hold values from 0.5 to 1.5
- moe_gain: float32 [2048], replicated, may hold values from 0.5 to 1.5
- qkv_train: float32 [2048, 3, 2048], P('seq', None, 'tp'), may hold values from -0.125 to 0.125
- out_train: float32 [2048, 2048], P('seq', 'tp'), may hold values from -0.125 to 0.125
- router: bfloat16 [2048, 64], replicated, may hold values from -0.125 to 0.125
- routes: int32 [8192, 6], P('seq'), may hold values from 0 to 63, all different within a row; in each aligned block of 256 rows (0 to 255, 256 to 511, ...) at most 32 rows name the same one
- handed_half: int32 [32], replicated, may hold values from 0 to 1
- fresh_gu: float32 [32, 1408, 2, 2048], P('seq', 'tp'), may hold values from -0.125 to 0.125
- fresh_down: float32 [32, 1408, 2048], P('seq', 'tp'), may hold values from -0.15625 to 0.15625
- server_gu: bfloat16 [32, 2816, 2, 2048], P('seq', 'tp'), may hold values from -0.125 to 0.125
- server_down: bfloat16 [32, 2816, 2048], P('seq', 'tp'), may hold values from -0.15625 to 0.15625
Outputs:
- layer_out: bfloat16 [8192, 2048], P('seq', 'tp')
Inputs may be any that keep to these rules, and one draw needn't show every extreme that they name: `ctx_len`: some request has exactly 12288 cached positions and some has none. `cache_pos`: -1 marks an empty slot. With a context length L of at most 4096, slot s holds position s for s < L. With a longer context, slots below 4 hold positions 0 to 3 and the other slots hold positions L - 4092 to L - 1, each once. `routes`: each row names 6 different experts; in the rows of one request no expert is named by more than 32 rows, and in every draw some expert by exactly 32. `cache_kv`: keys already carry their position's rotation.
All inputs are finite; a program needn't handle non-finite values.
Results may differ from a plain program's by a relative error of at most 0.025.
Values may be sent and summed in bfloat16 or wider, within the bound.
A program may use at most 128 MiB of HBM per device.

v0:
```python
import jax
import jax.numpy as jnp
from jax import lax
from jax.sharding import PartitionSpec as P

HEAD_DIM = 128
SINK = 4
WIN = 4096


def swapped(array, axis, apart):
    return lax.ppermute(array, axis, [(i, i ^ 1 << apart) for i in range(lax.axis_size(axis))])


def normed(field, gain_vec):
    values_in = field.astype(jnp.float32)
    inv_rms = lax.rsqrt(jnp.mean(values_in * values_in, axis=-1, keepdims=True) + 1e-06)
    return (values_in * inv_rms * gain_vec).astype(jnp.bfloat16)


def rotate(field, positions):
    half_dim = field.shape[-1] // 2
    frequency = 10000.0 ** (-jnp.arange(half_dim, dtype=jnp.float32) / half_dim)
    angles = positions.astype(jnp.float32)[:, None] * frequency[None, :]
    cosine = jnp.cos(angles)[:, None, :]
    sine = jnp.sin(angles)[:, None, :]
    first_half = field[..., :half_dim]
    second_half = field[..., half_dim:]
    return jnp.concatenate(
        [first_half * cosine - second_half * sine, second_half * cosine + first_half * sine],
        axis=-1,
    )


def attend(queries, keys_new, values_new, cache_keys, cache_values, slot_pos, context):
    new_count = queries.shape[0]
    key_all = jnp.concatenate([cache_keys, keys_new], axis=0)
    value_all = jnp.concatenate([cache_values, values_new], axis=0)
    scores = jnp.einsum(
        "qhd,khd->hqk", queries, key_all, preferred_element_type=jnp.float32
    ) / jnp.sqrt(jnp.float32(HEAD_DIM))
    token_ids = jnp.arange(new_count, dtype=jnp.int32)
    positions = context + token_ids
    cache_ok = (slot_pos[None, :] >= 0) & (
        (slot_pos[None, :] < SINK) | (positions[:, None] - slot_pos[None, :] < WIN)
    )
    new_ok = token_ids[None, :] <= token_ids[:, None]
    allowed = jnp.concatenate([cache_ok, new_ok], axis=1)
    scores = jnp.where(allowed[None], scores, jnp.float32(-1e30))
    row_top = jnp.max(scores, axis=-1, keepdims=True)
    weights = jnp.exp(scores - row_top)
    row_total = jnp.sum(weights, axis=-1, keepdims=True)
    probability = (weights / row_total).astype(jnp.bfloat16)
    return jnp.einsum(
        "hqk,khd->qhd", probability, value_all, preferred_element_type=jnp.float32
    ).astype(jnp.bfloat16)


def body(
    tokens,
    ctx_len,
    cache_kv,
    cache_pos,
    attn_gain,
    moe_gain,
    qkv_train,
    out_train,
    router,
    routes,
    handed_half,
    fresh_gu,
    fresh_down,
    server_gu,
    server_down,
):
    seq_count = lax.axis_size("seq")
    tp_place = lax.axis_index("tp")
    seq_place = lax.axis_index("seq")
    full_tokens = lax.all_gather(tokens, "tp", axis=1, tiled=True)
    tok_rows = full_tokens.shape[0]
    model_width = full_tokens.shape[1]
    qkv_all, out_all = (
        lax.all_gather(qkv_train.astype(jnp.bfloat16), "seq", axis=0, tiled=True),
        lax.all_gather(out_train.astype(jnp.bfloat16), "seq", axis=0, tiled=True),
    )
    local_width = qkv_all.shape[2]
    heads_here = local_width // HEAD_DIM
    normed_x = normed(full_tokens, attn_gain)
    projected = jnp.dot(
        normed_x, qkv_all.reshape(model_width, 3 * local_width), preferred_element_type=jnp.float32
    )
    projected = projected.reshape(tok_rows, 3, heads_here, HEAD_DIM)
    context = ctx_len[0]
    positions = context + jnp.arange(tok_rows, dtype=jnp.int32)
    queries = rotate(projected[:, 0], positions).astype(jnp.bfloat16)
    keys_new = rotate(projected[:, 1], positions).astype(jnp.bfloat16)
    values_new = projected[:, 2].astype(jnp.bfloat16)
    slot_count = cache_kv.shape[1]
    cached = cache_kv[0].reshape(slot_count, 2, heads_here, HEAD_DIM)
    mixed_heads = attend(
        queries, keys_new, values_new, cached[:, 0], cached[:, 1], cache_pos[0], context
    )
    mixed_heads = mixed_heads.reshape(tok_rows, local_width)
    partial_out = lax.dot_general(
        mixed_heads, out_all, (((1,), (1,)), ((), ())), preferred_element_type=jnp.float32
    )
    attn_total = lax.psum(partial_out.astype(jnp.bfloat16), "tp").astype(jnp.float32)
    hidden_state = (full_tokens.astype(jnp.float32) + attn_total).astype(jnp.bfloat16)
    moe_in = normed(hidden_state, moe_gain)
    logits = jnp.dot(moe_in, router, preferred_element_type=jnp.float32)
    gate_values = jax.nn.sigmoid(jnp.take_along_axis(logits, routes, axis=1))
    expert_count = router.shape[1]
    top_count = routes.shape[1]
    capacity = tok_rows // 8
    flat_routes = routes.reshape(-1)
    onehot = (flat_routes[:, None] == jnp.arange(expert_count, dtype=jnp.int32)[None, :]).astype(
        jnp.int32
    )
    before = jnp.cumsum(onehot, axis=0) - onehot
    slot_rank = jnp.sum(before * onehot, axis=1)
    slot_index = flat_routes * capacity + slot_rank
    repeated = jnp.repeat(moe_in, top_count, axis=0)
    outgoing = (
        jnp.zeros((expert_count * capacity, model_width), jnp.bfloat16).at[slot_index].set(repeated)
    )
    per_device = expert_count // seq_count
    pair_count = per_device // 2
    outgoing = outgoing.reshape(seq_count, per_device, capacity, model_width)
    arrived = lax.all_to_all(outgoing, "seq", split_axis=0, concat_axis=0, tiled=True)
    parity = tp_place % 2
    own_gu = fresh_gu.astype(jnp.bfloat16)
    own_down = fresh_down.astype(jnp.bfloat16)
    other_gu, other_down = swapped((own_gu, own_down), "tp", 0)
    lower_first = parity == 0
    group_gu = jnp.where(
        lower_first,
        jnp.concatenate([own_gu, other_gu], axis=1),
        jnp.concatenate([other_gu, own_gu], axis=1),
    )
    group_down = jnp.where(
        lower_first,
        jnp.concatenate([own_down, other_down], axis=1),
        jnp.concatenate([other_down, own_down], axis=1),
    )
    local_half = lax.dynamic_slice_in_dim(handed_half, seq_place * pair_count, pair_count, 0)
    use_fresh = local_half == parity
    weights_gu = jnp.where(use_fresh[:, None, None, None], group_gu, server_gu)
    weights_down = jnp.where(use_fresh[:, None, None], group_down, server_down)
    arrived_pairs = arrived.reshape(seq_count, pair_count, 2, capacity, model_width)
    mine = lax.dynamic_index_in_dim(arrived_pairs, parity, 2, keepdims=False)
    pre_act = jnp.einsum("sqcd,qfgd->sqcgf", mine, weights_gu, preferred_element_type=jnp.float32)
    activated = (jax.nn.silu(pre_act[..., 0, :]) * pre_act[..., 1, :]).astype(jnp.bfloat16)
    partial_y = jnp.einsum(
        "sqcf,qfd->sqcd", activated, weights_down, preferred_element_type=jnp.float32
    )
    selector = (jnp.arange(2, dtype=jnp.int32) == parity).astype(jnp.float32)
    placed = partial_y[:, :, None] * selector[None, None, :, None, None]
    placed = placed.reshape(seq_count, per_device, capacity, model_width)
    summed = lax.psum_scatter(placed.astype(jnp.bfloat16), "tp", scatter_dimension=3, tiled=True)
    returned = lax.all_to_all(summed, "seq", split_axis=0, concat_axis=0, tiled=True)
    part_width = returned.shape[3]
    flat_back = returned.reshape(expert_count * capacity, part_width)
    picked = flat_back[slot_index].reshape(tok_rows, top_count, part_width)
    combined = jnp.sum(gate_values[:, :, None] * picked.astype(jnp.float32), axis=1)
    residual = lax.dynamic_slice_in_dim(hidden_state, tp_place * part_width, part_width, 1)
    return (residual.astype(jnp.float32) + combined).astype(jnp.bfloat16)


def solution(mesh):
    placed = (
        P("seq", "tp"),
        P("seq"),
        P("seq", None, None, "tp"),
        P("seq", None),
        P(),
        P(),
        P("seq", None, "tp"),
        P("seq", "tp"),
        P(),
        P("seq", None),
        P(),
        P("seq", "tp", None, None),
        P("seq", "tp", None),
        P("seq", "tp", None, None),
        P("seq", "tp", None),
    )
    return jax.shard_map(
        body, mesh=mesh, in_specs=placed, out_specs=P("seq", "tp"), check_vma=False
    )
```

profile of v0, /device:TPU:4, one launch (start us, length us, event | category | flops | bytes accessed | tf_op | source)
XLA Modules:
  0.0 695.0 jit_solution(49394141733792327)
XLA Ops:
  6.5 0.7 all-gather.4.cloned.1.call-update
  7.3 1.6 convert_element_type.97
  9.0 1.4 convert_element_type.103
  11.2 0.8 compare_reduce_fusion.1
  12.0 11.2 %copy.54 = bf16[1,4096,2,256]{1,3,2,0:T(8,128)(2,1)} copy(bf16[1,4096,2,256]{3,2,1,0:T(2,128)(2,1)} %param.17) | data formatting | bytes 8388608 | tf_op args[2]
  23.2 4.0 slice_bitcast_fusion
  27.2 2.4 copy.73
  29.6 0.3 multiply_cosine_fusion
  29.9 1.0 fusion.9
  31.1 20.9 %all-gather.4.cloned.1.call-done = bf16[256,2048]{1,0:T(8,128)(2,1)} async-done(((bf16[256,256]{1,0:T(8,128)(2,1)}), bf16[256,2048]{1,0:T(8,128)(2,1)}) %all-gather.4.cloned.1.call-update) | async-done | bytes 1048592 | tf_op jit(solution)/shard_map/all_gather | solution.py:79
  52.0 1.5 fusion.21
  53.6 83.9 %all-gather.6.cloned.1.call-done = bf16[2048,3,256]{2,0,1:T(8,128)(2,1)} async-done(((bf16[64,3,256]{2,0,1:T(8,128)(2,1)}), bf16[2048,3,256]{2,0,1:T(8,128)(2,1)}) %all-gather.6.cloned.1.call-update) | async-done | bytes 3145744 | tf_op jit(solution)/shard_map/all_gather | solution.py:83
  137.5 4.7 copy.55
  142.2 3.0 fusion.45
  145.3 0.7 copy-done.4
  146.1 0.1 copy.57
  146.2 5.3 multiply_select_fusion
  151.5 1.0 fusion.55
  152.5 2.3 exponential_reduce_fusion
  154.7 3.4 fusion.41
  158.2 56.9 %all-gather.8.cloned.1.call-done = bf16[2048,256]{1,0:T(8,128)(2,1)} async-done(((bf16[64,256]{1,0:T(8,128)(2,1)}), bf16[2048,256]{1,0:T(8,128)(2,1)}) %all-gather.8.cloned.1.call-update) | async-done | bytes 1048592 | tf_op jit(solution)/shard_map/all_gather | solution.py:84
  215.1 2.7 convolution_convert_fusion
  217.8 0.1 copy.63
  217.9 0.1 eq.53
  218.1 0.1 eq.49
  218.3 18.3 %reduce-window.6 = s32[64,12,128]{2,1,0:T(8,128)S(1)} reduce-window(s32[64,12,128]{2,1,0:T(8,128)S(1)} %fusion.51, s32[]{:T(128)} %constant.29.clone.1), window={size=1x1x128 pad=0_0x0_0x127_0}, to_apply=%region_5.6 | reduce-window | flops 12484608 | bytes 786436 | tf_op jit(solution)/shard_map/reduce-window
  236.6 0.2 slice.66
  236.8 0.3 copy.65
  237.1 0.1 copy.66
  237.2 0.1 copy.62
  237.3 0.1 mul.207
  237.5 0.2 broadcast_add_fusion
  237.7 0.2 fusion.54
  237.9 60.7 %all-reduce.2.cloned.1.call-done = bf16[256,2048]{1,0:T(8,128)(2,1)} async-done(((bf16[256,2048]{1,0:T(8,128)(2,1)}), bf16[256,2048]{1,0:T(8,128)(2,1)}) %all-reduce.2.cloned.1.call-update) | async-done | bytes 1048592 | tf_op jit(solution)/shard_map/psum | solution.py:107
  298.6 1.7 fusion.18
  300.4 1.0 copy-done.1
  301.3 0.3 fusion.20
  301.6 4.6 broadcast_in_dim.42
  306.3 11.1 %reshape.346 = bf16[1536,2048]{1,0:T(8,128)(2,1)} reshape(bf16[256,6,2048]{2,1,0:T(8,128)(2,1)} %broadcast_in_dim.42) | data formatting | bytes 12582912 | tf_op jit(solution)/shard_map/reshape | solution.py:122
  317.3 15.1 %scatter_custom_fusion = bf16[2048,2048]{1,0:T(8,128)(2,1)} fusion(s32[1536]{0:T(1024)S(1)} %fusion.59, bf16[1536,2048]{1,0:T(8,128)(2,1)} %reshape.346, bf16[]{:T(256)} %constant.85.clone.1), kind=kCustom, calls=%fused_computation.17 | custom fusion | bytes 8389120 | tf_op jit(solution)/shard_map/scatter | solution.py:124
  332.4 10.2 %all-to-all-start = ((bf16[32,2,32,2048]{3,2,1,0:T(8,128)(2,1)}), bf16[32,2,32,2048]{3,2,1,0:T(8,128)(2,1)}, u32[]{:S(2)}, u32[]{:S(2)}) async-start(bf16[32,2,32,2048]{3,2,1,0:T(8,128)(2,1)} %bitcast.87), calls=%async_computation | async-start | bytes 16777216 | tf_op jit(solution)/shard_map/all_to_all | solution.py:129
  342.6 0.3 reduce-scatter.2.cloned.1.call-start
  342.9 3.3 convert_element_type.111
  346.4 2.1 collective-permute-start
  348.5 0.6 dynamic_slice.9
  349.6 31.2 %collective-permute-done.1 = bf16[1,176,2,2048]{3,2,1,0:T(2,128)(2,1)} collective-permute-done((bf16[1,176,2,2048]{3,2,1,0:T(2,128)(2,1)S(1)}, bf16[1,176,2,2048]{3,2,1,0:T(2,128)(2,1)}, u32[]{:S(2)}, u32[]{:S(2)}) %collective-permute-start.1) | collective-permute-done | bytes 1441824 | tf_op jit(solution)/shard_map/ppermute | solution.py:12
  380.8 16.0 %fusion.10 = bf16[352,2,2048,1]{2,1,0,3:T(2,128)(2,1)} fusion(bf16[1,352,2,2048]{3,2,1,0:T(2,128)(2,1)} %param.28, pred[]{:T(512)} %bitcast.17, pred[]{:T(512)S(6)} %eq.48, bf16[1,176,2,2048]{3,2,1,0:T(2,128)(2,1)} %collective-permute-done.1, bf16[1,176,2,2048]{3,2,1,0:T(2,128)(2,1)S(1)} %convert_element_type.111), kind=kLoop, calls=%fused_computation.25 | loop fusion | flops 5767168 | bytes 8650754 | tf_op jit(solution)/shard_map/reshape.10
  396.8 128.1 %all-to-all-done = bf16[32,2,32,2048]{3,2,1,0:T(8,128)(2,1)} async-done(((bf16[32,2,32,2048]{3,2,1,0:T(8,128)(2,1)}), bf16[32,2,32,2048]{3,2,1,0:T(8,128)(2,1)}, u32[]{:S(2)}, u32[]{:S(2)}) %all-to-all-start) | async-done | bytes 8388640 | tf_op jit(solution)/shard_map/all_to_all | solution.py:129
  524.9 7.3 %fusion.25 = f32[32,1,32,2,352]{4,2,0,3,1:T(8,128)S(1)} fusion(bf16[32,2,32,2048]{3,2,1,0:T(8,128)(2,1)} %all-to-all-done, s32[]{:T(128)S(6)} %select_n.95, bf16[352,2,2048,1]{2,1,0,3:T(2,128)(2,1)} %fusion.10), kind=kOutput, calls=%fused_computation.45 | convolution fusion | flops 2952790016 | bytes 9961476 | tf_op jit(solution)/shard_map/sqcd,qfgd->sqcgf/dot_general | solution.py:151
  532.2 7.0 %convolution_bitcast_fusion = f32[32,32,2048]{2,1,0:T(8,128)} fusion(bf16[1,352,2048]{2,1,0:T(8,128)(2,1)S(1)} %copy-done.8, bf16[1,176,2048]{2,1,0:T(8,128)(2,1)} %collective-permute-done, bf16[1,176,2048]{2,1,0:T(8,128)(2,1)S(1)} %convert_element_type.110, pred[]{:T(512)S(6)} %eq.48, pred[]{:T(512)} %bitcast.17, f32[32,1,32,2,352]{4,2,0,3,1:T(8,128)S(1)} %fusion.25), kind=kOutput, calls=%fused_computation.13 | convolution fusion | flops 1485766656 | bytes 14155778 | tf_op jit(solution)/shard_map/sqcf,qfd->sqcd/dot_general | solution.py:153
  539.2 8.5 %multiply_convert_fusion = bf16[32,2,32,2048]{3,2,1,0:T(8,128)(2,1)} fusion(f32[2]{0:T(128)S(1)} %compare_convert_fusion, f32[32,32,2048]{2,1,0:T(8,128)} %convolution_bitcast_fusion), kind=kLoop, calls=%fused_computation.4 | loop fusion | flops 8388608 | bytes 16777224 | tf_op jit(solution)/shard_map/convert_element_type | solution.py:159
  547.8 94.4 %reduce-scatter.2.cloned.1.call-done = bf16[32,2,32,256]{3,2,1,0:T(8,128)(2,1)} async-done(((bf16[32,2,32,2048]{3,2,1,0:T(8,128)(2,1)}), bf16[32,2,32,256]{3,2,1,0:T(8,128)(2,1)}) %reduce-scatter.2.cloned.1.call-update) | async-done | bytes 1048592 | tf_op jit(solution)/shard_map/reduce_scatter | solution.py:159
  642.1 10.1 %all-to-all-start.1 = ((bf16[32,2,32,256]{3,2,1,0:T(8,128)(2,1)}), bf16[32,2,32,256]{3,2,1,0:T(8,128)(2,1)S(1)}, u32[]{:S(2)}, u32[]{:S(2)}) async-start(bf16[32,2,32,256]{3,2,1,0:T(8,128)(2,1)} %reduce-scatter.2.cloned.1.call-done), calls=%async_computation.2 | async-start | bytes 2097152 | tf_op jit(solution)/shard_map/all_to_all | solution.py:160
  652.3 0.1 copy.59
  652.5 0.1 reshape.336
  652.6 0.4 fusion.67
  653.1 12.7 %gather_fusion.1 = f32[1536]{0:T(1024)S(1)} fusion(f32[256,64]{0,1:T(8,128)S(1)} %fusion.67, s32[1536]{0:T(1024)S(1)} %reshape.336), kind=kCustom, calls=%fused_computation.1 | custom fusion | bytes 24576 | tf_op jit(solution)/shard_map/jit(take_along_axis)/gather | solution.py:111
  665.8 0.1 reshape.339
  666.0 0.1 copy.61
  666.2 15.0 %all-to-all-done.1 = bf16[32,2,32,256]{3,2,1,0:T(8,128)(2,1)S(1)} async-done(((bf16[32,2,32,256]{3,2,1,0:T(8,128)(2,1)}), bf16[32,2,32,256]{3,2,1,0:T(8,128)(2,1)S(1)}, u32[]{:S(2)}, u32[]{:S(2)}) %all-to-all-start.1) | async-done | bytes 1048608 | tf_op jit(solution)/shard_map/all_to_all | solution.py:160
  681.2 4.8 gather_fusion
  686.0 0.2 reshape.327
  686.2 0.7 multiply_reduce_fusion
  686.9 1.6 add_convert_fusion
  (49 shorter events, 0.9 us)
Async XLA Ops:
  6.5 646.1 %copy-start = (bf16[2048,64]{0,1:T(8,128)(2,1)S(1)}, bf16[2048,64]{0,1:T(8,128)(2,1)}, u32[]{:S(2)}) copy-start(bf16[2048,64]{0,1:T(8,128)(2,1)} %param.23) | copy-start | bytes 786436
  6.5 45.5 %all-gather.4.cloned.1.call-start = ((), (), s32[]{:S(2)}) async-start(), calls=%async_computation.3 | async-start | bytes 1179648 | tf_op jit(solution)/shard_map/all_gather | solution.py:79
  7.3 130.2 %all-gather.6.cloned.1.call-start = ((), (), s32[]{:S(2)}) async-start(), calls=%async_computation.4 | async-start | bytes 3244032 | tf_op jit(solution)/shard_map/all_gather | solution.py:83
  8.9 206.1 %all-gather.8.cloned.1.call-start = ((), (), s32[]{:S(2)}) async-start(), calls=%async_computation.5 | async-start | bytes 1081344 | tf_op jit(solution)/shard_map/all_gather | solution.py:84
  10.4 288.2 %all-reduce.2.cloned.1.call-start = ((), (), s32[]{:S(2)}) async-start(), calls=%async_computation.6 | async-start | bytes 2097152 | tf_op jit(solution)/shard_map/psum | solution.py:107
  27.2 2.8 copy-start.6
  53.5 88.7 %copy-start.2 = (bf16[256,2048]{1,0:T(8,128)(2,1)S(1)}, bf16[256,2048]{1,0:T(8,128)(2,1)}, u32[]{:S(2)}) copy-start(bf16[256,2048]{1,0:T(8,128)(2,1)} %all-gather.4.cloned.1.call-done) | copy-start | bytes 3145732
  53.5 88.6 %copy-start.9 = (f32[2048]{0:T(1024)S(1)}, f32[2048]{0:T(1024)}, u32[]{:S(2)}) copy-start(f32[2048]{0:T(1024)} %param.19) | copy-start | bytes 24580
  145.2 0.9 copy-start.4
  158.2 59.6 %copy-start.5 = (s32[256,6]{0,1:T(8,128)S(1)}, s32[256,6]{0,1:T(8,128)}, u32[]{:S(2)}) copy-start(s32[256,6]{0,1:T(8,128)} %param.24) | copy-start | bytes 18436
  236.8 64.6 %copy-start.7 = (f32[2048]{0:T(1024)S(1)}, f32[2048]{0:T(1024)}, u32[]{:S(2)}) copy-start(f32[2048]{0:T(1024)} %param.20) | copy-start | bytes 24580
  300.3 1.0 copy-start.1
  332.4 192.5 %all-to-all-start = ((bf16[32,2,32,2048]{3,2,1,0:T(8,128)(2,1)}), bf16[32,2,32,2048]{3,2,1,0:T(8,128)(2,1)}, u32[]{:S(2)}, u32[]{:S(2)}) async-start(bf16[32,2,32,2048]{3,2,1,0:T(8,128)(2,1)} %bitcast.87), calls=%async_computation | async-start | bytes 16777216 | tf_op jit(solution)/shard_map/all_to_all | solution.py:129
  342.6 5.9 copy-start.10
  342.6 299.6 %reduce-scatter.2.cloned.1.call-start = ((), (), s32[]{:S(2)}) async-start(), calls=%async_computation.7 | async-start | bytes 9437184 | tf_op jit(solution)/shard_map/reduce_scatter | solution.py:159
  342.9 3.4 copy-start.3
  346.1 34.6 %collective-permute-start.1 = (bf16[1,176,2,2048]{3,2,1,0:T(2,128)(2,1)S(1)}, bf16[1,176,2,2048]{3,2,1,0:T(2,128)(2,1)}, u32[]{:S(2)}, u32[]{:S(2)}) collective-permute-start(bf16[1,176,2,2048]{3,2,1,0:T(2,128)(2,1)S(1)} %convert_element_type.111), channel_id=1, source_target_pairs={{0,1},{1,0},{2,3},{3,2},{4,5},{5,4},{6,7},{7,6},{8,9},{9,8},{10,11... | collective-permute-start | bytes 4325384 | tf_op jit(solution)/shard_map/ppermute | solution.py:12
  346.4 185.8 %collective-permute-start = (bf16[1,176,2048]{2,1,0:T(8,128)(2,1)S(1)}, bf16[1,176,2048]{2,1,0:T(8,128)(2,1)}, u32[]{:S(2)}, u32[]{:S(2)}) collective-permute-start(bf16[1,176,2048]{2,1,0:T(8,128)(2,1)S(1)} %convert_element_type.110), channel_id=1, source_target_pairs={{0,1},{1,0},{2,3},{3,2},{4,5},{5,4},{6,7},{7,6},{8,9},{9,8},{10,11... | collective-permute-start | bytes 2162696 | tf_op jit(solution)/shard_map/ppermute | solution.py:12
  396.8 135.4 %copy-start.8 = (bf16[1,352,2048]{2,1,0:T(8,128)(2,1)S(1)}, bf16[1,352,2048]{2,1,0:T(8,128)(2,1)}, u32[]{:S(2)}) copy-start(bf16[1,352,2048]{2,1,0:T(8,128)(2,1)} %param.29) | copy-start | bytes 4325380
  642.1 39.1 %all-to-all-start.1 = ((bf16[32,2,32,256]{3,2,1,0:T(8,128)(2,1)}), bf16[32,2,32,256]{3,2,1,0:T(8,128)(2,1)S(1)}, u32[]{:S(2)}, u32[]{:S(2)}) async-start(bf16[32,2,32,256]{3,2,1,0:T(8,128)(2,1)} %reduce-scatter.2.cloned.1.call-done), calls=%async_computation.2 | async-start | bytes 2097152 | tf_op jit(solution)/shard_map/all_to_all | solution.py:160
Sparse Core Ops, SparseCore 0:
  9.1 42.8 all-gather.3
  54.8 82.6 all-gather.5
  140.3 74.7 all-gather.7
  217.9 80.6 all-reduce.1
  547.9 94.2 reduce-scatter.1
where the time goes:
time: 696 us; the launch traced here: 695 us
  waiting for transfers between devices  492 us (71%)
  local copies, waits for them, and re-layouts  76.1 us (11%)
  other arithmetic  60.2 us (9%)
  matrix products  29.2 us (4%)
  starting transfers between devices  22.9 us (3%)
  between operations  14.8 us (2%)
    all_to_all x1, waiting for transfers between devices, body(): lax.all_to_all(outgoing, 'seq', split_axis=0, concat_axis=0, tiled=True)  128 us
    reduce_scatter x1, waiting for transfers between devices, body(): lax.psum_scatter(placed.astype(jnp.bfloat16), 'tp', scatter_dimension=3,...  94.4 us
    all_gather x1, waiting for transfers between devices, body(): lax.all_gather(qkv_train.astype(jnp.bfloat16), 'seq', axis=0, tiled=True)  83.9 us
    psum x1, waiting for transfers between devices, body(): lax.psum(partial_out.astype(jnp.bfloat16), 'tp').astype(jnp.float32)  60.7 us
    all_gather x1, waiting for transfers between devices, body(): lax.all_gather(out_train.astype(jnp.bfloat16), 'seq', axis=0, tiled=True)  56.9 us
    another operation x5, other arithmetic  34.6 us
    ppermute x2, waiting for transfers between devices, swapped(): lax.ppermute(array, axis, [(i, i ^ 1 << apart) for i in range(lax.axis_si...  31.2 us
    all_gather x1, waiting for transfers between devices, body(): full_tokens = lax.all_gather(tokens, 'tp', axis=1, tiled=True)  20.9 us
  transfers between devices with their start and end apart: 9, of which 8 were waited for; matrix products, arithmetic and copies ran while one was open for 15% of the time, Pallas kernels for 0%

commit v1 on v0

--- a/solution.py
+++ b/solution.py
@@ -104,7 +104,9 @@
     partial_out = lax.dot_general(
         mixed_heads, out_all, (((1,), (1,)), ((), ())), preferred_element_type=jnp.float32
     )
-    attn_total = lax.psum(partial_out.astype(jnp.bfloat16), "tp").astype(jnp.float32)
+    attn_total = jnp.sum(lax.all_gather(partial_out.astype(jnp.bfloat16), "tp"), axis=0).astype(
+        jnp.float32
+    )
     hidden_state = (full_tokens.astype(jnp.float32) + attn_total).astype(jnp.bfloat16)
     moe_in = normed(hidden_state, moe_gain)
     logits = jnp.dot(moe_in, router, preferred_element_type=jnp.float32)

time: 696 us -> 720 us (1.034); the launches traced: 695 us -> 711 us
  waiting for transfers between devices: 492 us -> 503 us
    all_gather x0 -> x1, waiting for transfers between devices: none -> 72.7 us  [body(): lax.all_gather(partial_out.astype(jnp.bfloat16), 'tp')]
    psum x1 -> x0, waiting for transfers between devices: 60.7 us -> none  [body(): lax.psum(partial_out.astype(jnp.bfloat16), 'tp').astype(jnp.float32)]
where the time goes in v1:
time: 720 us; the launch traced here: 711 us
  waiting for transfers between devices  503 us (70%)
  local copies, waits for them, and re-layouts  76.2 us (11%)
  other arithmetic  64.5 us (9%)
  matrix products  29.2 us (4%)
  starting transfers between devices  22.9 us (3%)
  between operations  15 us (2%)
    all_to_all x1, waiting for transfers between devices, body(): lax.all_to_all(outgoing, 'seq', split_axis=0, concat_axis=0, tiled=True)  128 us
    reduce_scatter x1, waiting for transfers between devices, body(): lax.psum_scatter(placed.astype(jnp.bfloat16), 'tp', scatter_dimension=3,...  93.5 us
    all_gather x1, waiting for transfers between devices, body(): lax.all_gather(qkv_train.astype(jnp.bfloat16), 'seq', axis=0, tiled=True)  83.9 us
    all_gather x1, waiting for transfers between devices, body(): lax.all_gather(partial_out.astype(jnp.bfloat16), 'tp')  72.7 us
    all_gather x1, waiting for transfers between devices, body(): lax.all_gather(out_train.astype(jnp.bfloat16), 'seq', axis=0, tiled=True)  56.9 us
    another operation x5, other arithmetic  34.9 us
    ppermute x2, waiting for transfers between devices, swapped(): lax.ppermute(array, axis, [(i, i ^ 1 << apart) for i in range(lax.axis_si...  31.2 us
    all_gather x1, waiting for transfers between devices, body(): full_tokens = lax.all_gather(tokens, 'tp', axis=1, tiled=True)  20.9 us
  transfers between devices with their start and end apart: 9, of which 8 were waited for; matrix products, arithmetic and copies ran while one was open for 15% of the time, Pallas kernels for 0%

profile of v1, /device:TPU:4, one launch (start us, length us, event | category | flops | bytes accessed | tf_op | source)
XLA Modules:
  0.0 711.1 jit_solution(16326851387398706127)
XLA Ops:
  6.5 0.7 all-gather.6.cloned.1.call-update
  7.3 1.6 convert_element_type.99
  9.0 1.4 convert_element_type.105
  11.2 0.8 compare_reduce_fusion.1
  12.0 11.2 %copy.54 = bf16[1,4096,2,256]{1,3,2,0:T(8,128)(2,1)} copy(bf16[1,4096,2,256]{3,2,1,0:T(2,128)(2,1)} %param.17) | data formatting | bytes 8388608 | tf_op args[2]
  23.2 4.0 slice_bitcast_fusion
  27.2 2.4 copy.73
  29.6 0.3 multiply_cosine_fusion
  29.9 1.0 fusion.9
  31.1 20.9 %all-gather.6.cloned.1.call-done = bf16[256,2048]{1,0:T(8,128)(2,1)} async-done(((bf16[256,256]{1,0:T(8,128)(2,1)}), bf16[256,2048]{1,0:T(8,128)(2,1)}) %all-gather.6.cloned.1.call-update) | async-done | bytes 1048592 | tf_op jit(solution)/shard_map/all_gather | solution.py:79
  52.0 1.5 fusion.21
  53.6 83.9 %all-gather.8.cloned.1.call-done = bf16[2048,3,256]{2,0,1:T(8,128)(2,1)} async-done(((bf16[64,3,256]{2,0,1:T(8,128)(2,1)}), bf16[2048,3,256]{2,0,1:T(8,128)(2,1)}) %all-gather.8.cloned.1.call-update) | async-done | bytes 3145744 | tf_op jit(solution)/shard_map/all_gather | solution.py:83
  137.5 4.7 copy.55
  142.2 3.0 fusion.45
  145.3 0.7 copy-done.4
  146.1 0.1 copy.57
  146.2 5.3 multiply_select_fusion
  151.5 1.0 fusion.55
  152.5 2.3 exponential_reduce_fusion
  154.7 3.4 fusion.41
  158.2 56.9 %all-gather.10.cloned.1.call-done = bf16[2048,256]{1,0:T(8,128)(2,1)} async-done(((bf16[64,256]{1,0:T(8,128)(2,1)}), bf16[2048,256]{1,0:T(8,128)(2,1)}) %all-gather.10.cloned.1.call-update) | async-done | bytes 1048592 | tf_op jit(solution)/shard_map/all_gather | solution.py:84
  215.1 2.8 convolution_convert_fusion
  217.9 0.1 copy.63
  218.0 0.1 eq.53
  218.2 0.1 eq.49
  218.3 18.6 %reduce-window.6 = s32[64,12,128]{2,1,0:T(8,128)S(1)} reduce-window(s32[64,12,128]{2,1,0:T(8,128)S(1)} %fusion.51, s32[]{:T(128)} %constant.36.clone.1), window={size=1x1x128 pad=0_0x0_0x127_0}, to_apply=%region_5.6 | reduce-window | flops 12484608 | bytes 786436 | tf_op jit(solution)/shard_map/reduce-window
  236.9 0.2 slice.66
  237.1 0.3 copy.65
  237.4 0.1 copy.66
  237.5 0.1 copy.62
  237.7 0.1 mul.207
  237.8 0.2 broadcast_add_fusion
  238.0 0.2 fusion.54
  238.3 72.7 %all-gather.12.cloned.1.call-done = bf16[2048,2048]{1,0:T(8,128)(2,1)} async-done(((bf16[256,2048]{1,0:T(8,128)(2,1)}), bf16[2048,2048]{1,0:T(8,128)(2,1)}) %all-gather.12.cloned.1.call-update) | async-done | bytes 8388624 | tf_op jit(solution)/shard_map/all_gather | solution.py:107
  310.9 5.2 reduce_sum.61
  316.2 0.5 fusion.18
  316.7 1.0 copy-done.1
  317.6 0.3 fusion.20
  318.0 4.6 broadcast_in_dim.42
  322.6 11.1 %reshape.346 = bf16[1536,2048]{1,0:T(8,128)(2,1)} reshape(bf16[256,6,2048]{2,1,0:T(8,128)(2,1)} %broadcast_in_dim.42) | data formatting | bytes 12582912 | tf_op jit(solution)/shard_map/reshape | solution.py:124
  333.6 15.2 %scatter_custom_fusion = bf16[2048,2048]{1,0:T(8,128)(2,1)} fusion(s32[1536]{0:T(1024)S(1)} %fusion.59, bf16[1536,2048]{1,0:T(8,128)(2,1)} %reshape.346, bf16[]{:T(256)} %constant.74.clone.1), kind=kCustom, calls=%fused_computation.17 | custom fusion | bytes 8389120 | tf_op jit(solution)/shard_map/scatter | solution.py:126
  348.9 10.2 %all-to-all-start = ((bf16[32,2,32,2048]{3,2,1,0:T(8,128)(2,1)}), bf16[32,2,32,2048]{3,2,1,0:T(8,128)(2,1)}, u32[]{:S(2)}, u32[]{:S(2)}) async-start(bf16[32,2,32,2048]{3,2,1,0:T(8,128)(2,1)} %bitcast.88), calls=%async_computation | async-start | bytes 16777216 | tf_op jit(solution)/shard_map/all_to_all | solution.py:131
  359.2 3.3 convert_element_type.113
  362.6 2.1 collective-permute-start
  364.7 0.6 dynamic_slice.9
  365.9 31.2 %collective-permute-done.1 = bf16[1,176,2,2048]{3,2,1,0:T(2,128)(2,1)} collective-permute-done((bf16[1,176,2,2048]{3,2,1,0:T(2,128)(2,1)S(1)}, bf16[1,176,2,2048]{3,2,1,0:T(2,128)(2,1)}, u32[]{:S(2)}, u32[]{:S(2)}) %collective-permute-start.1) | collective-permute-done | bytes 1441824 | tf_op jit(solution)/shard_map/ppermute | solution.py:12
  397.1 16.0 %fusion.10 = bf16[352,2,2048,1]{2,1,0,3:T(2,128)(2,1)} fusion(bf16[1,352,2,2048]{3,2,1,0:T(2,128)(2,1)} %param.28, pred[]{:T(512)} %bitcast.18, pred[]{:T(512)S(6)} %eq.48, bf16[1,176,2,2048]{3,2,1,0:T(2,128)(2,1)} %collective-permute-done.1, bf16[1,176,2,2048]{3,2,1,0:T(2,128)(2,1)S(1)} %convert_element_type.113), kind=kLoop, calls=%fused_computation.25 | loop fusion | flops 5767168 | bytes 8650754 | tf_op jit(solution)/shard_map/reshape.10
  413.1 128.3 %all-to-all-done = bf16[32,2,32,2048]{3,2,1,0:T(8,128)(2,1)} async-done(((bf16[32,2,32,2048]{3,2,1,0:T(8,128)(2,1)}), bf16[32,2,32,2048]{3,2,1,0:T(8,128)(2,1)}, u32[]{:S(2)}, u32[]{:S(2)}) %all-to-all-start) | async-done | bytes 8388640 | tf_op jit(solution)/shard_map/all_to_all | solution.py:131
  541.4 7.3 %fusion.25 = f32[32,1,32,2,352]{4,2,0,3,1:T(8,128)S(1)} fusion(bf16[32,2,32,2048]{3,2,1,0:T(8,128)(2,1)} %all-to-all-done, s32[]{:T(128)S(6)} %select_n.95, bf16[352,2,2048,1]{2,1,0,3:T(2,128)(2,1)} %fusion.10), kind=kOutput, calls=%fused_computation.45 | convolution fusion | flops 2952790016 | bytes 9961476 | tf_op jit(solution)/shard_map/sqcd,qfgd->sqcgf/dot_general | solution.py:153
  548.7 7.0 convolution_bitcast_fusion
  555.7 8.5 %multiply_convert_fusion = bf16[32,2,32,2048]{3,2,1,0:T(8,128)(2,1)} fusion(f32[2]{0:T(128)S(1)} %compare_convert_fusion, f32[32,32,2048]{2,1,0:T(8,128)} %convolution_bitcast_fusion), kind=kLoop, calls=%fused_computation.4 | loop fusion | flops 8388608 | bytes 16777224 | tf_op jit(solution)/shard_map/convert_element_type | solution.py:161
  564.3 93.5 %reduce-scatter.2.cloned.1.call-done = bf16[32,2,32,256]{3,2,1,0:T(8,128)(2,1)} async-done(((bf16[32,2,32,2048]{3,2,1,0:T(8,128)(2,1)}), bf16[32,2,32,256]{3,2,1,0:T(8,128)(2,1)}) %reduce-scatter.2.cloned.1.call-update) | async-done | bytes 1048592 | tf_op jit(solution)/shard_map/reduce_scatter | solution.py:161
  657.8 10.3 %all-to-all-start.1 = ((bf16[32,2,32,256]{3,2,1,0:T(8,128)(2,1)}), bf16[32,2,32,256]{3,2,1,0:T(8,128)(2,1)S(1)}, u32[]{:S(2)}, u32[]{:S(2)}) async-start(bf16[32,2,32,256]{3,2,1,0:T(8,128)(2,1)} %reduce-scatter.2.cloned.1.call-done), calls=%async_computation.2 | async-start | bytes 2097152 | tf_op jit(solution)/shard_map/all_to_all | solution.py:162
  668.1 0.1 copy.59
  668.3 0.1 reshape.336
  668.5 0.4 fusion.67
  668.9 12.7 %gather_fusion.1 = f32[1536]{0:T(1024)S(1)} fusion(f32[256,64]{0,1:T(8,128)S(1)} %fusion.67, s32[1536]{0:T(1024)S(1)} %reshape.336), kind=kCustom, calls=%fused_computation.1 | custom fusion | bytes 24576 | tf_op jit(solution)/shard_map/jit(take_along_axis)/gather | solution.py:113
  681.6 0.1 reshape.339
  681.9 0.1 copy.61
  682.0 15.0 %all-to-all-done.1 = bf16[32,2,32,256]{3,2,1,0:T(8,128)(2,1)S(1)} async-done(((bf16[32,2,32,256]{3,2,1,0:T(8,128)(2,1)}), bf16[32,2,32,256]{3,2,1,0:T(8,128)(2,1)S(1)}, u32[]{:S(2)}, u32[]{:S(2)}) %all-to-all-start.1) | async-done | bytes 1048608 | tf_op jit(solution)/shard_map/all_to_all | solution.py:162
  697.1 4.8 gather_fusion
  701.8 0.2 reshape.327
  702.0 0.7 multiply_reduce_fusion
  702.8 1.6 add_convert_fusion
  (50 shorter events, 0.9 us)
Async XLA Ops:
  6.5 661.9 %copy-start = (bf16[2048,64]{0,1:T(8,128)(2,1)S(1)}, bf16[2048,64]{0,1:T(8,128)(2,1)}, u32[]{:S(2)}) copy-start(bf16[2048,64]{0,1:T(8,128)(2,1)} %param.23) | copy-start | bytes 786436
  6.5 45.5 %all-gather.6.cloned.1.call-start = ((), (), s32[]{:S(2)}) async-start(), calls=%async_computation.3 | async-start | bytes 1179648 | tf_op jit(solution)/shard_map/all_gather | solution.py:79
  7.3 130.2 %all-gather.8.cloned.1.call-start = ((), (), s32[]{:S(2)}) async-start(), calls=%async_computation.4 | async-start | bytes 3244032 | tf_op jit(solution)/shard_map/all_gather | solution.py:83
  8.9 206.1 %all-gather.10.cloned.1.call-start = ((), (), s32[]{:S(2)}) async-start(), calls=%async_computation.5 | async-start | bytes 1081344 | tf_op jit(solution)/shard_map/all_gather | solution.py:84
  10.4 300.5 %all-gather.12.cloned.1.call-start = ((), (), s32[]{:S(2)}) async-start(), calls=%async_computation.7 | async-start | bytes 9437184 | tf_op jit(solution)/shard_map/all_gather | solution.py:107
  27.2 2.8 copy-start.6
  53.5 88.7 %copy-start.2 = (bf16[256,2048]{1,0:T(8,128)(2,1)S(1)}, bf16[256,2048]{1,0:T(8,128)(2,1)}, u32[]{:S(2)}) copy-start(bf16[256,2048]{1,0:T(8,128)(2,1)} %all-gather.6.cloned.1.call-done) | copy-start | bytes 3145732
  53.5 88.6 %copy-start.9 = (f32[2048]{0:T(1024)S(1)}, f32[2048]{0:T(1024)}, u32[]{:S(2)}) copy-start(f32[2048]{0:T(1024)} %param.19) | copy-start | bytes 24580
  145.2 0.9 copy-start.4
  158.2 59.7 %copy-start.5 = (s32[256,6]{0,1:T(8,128)S(1)}, s32[256,6]{0,1:T(8,128)}, u32[]{:S(2)}) copy-start(s32[256,6]{0,1:T(8,128)} %param.24) | copy-start | bytes 18436
  316.1 1.5 copy-start.7
  316.7 1.0 copy-start.1
  348.9 192.5 %all-to-all-start = ((bf16[32,2,32,2048]{3,2,1,0:T(8,128)(2,1)}), bf16[32,2,32,2048]{3,2,1,0:T(8,128)(2,1)}, u32[]{:S(2)}, u32[]{:S(2)}) async-start(bf16[32,2,32,2048]{3,2,1,0:T(8,128)(2,1)} %bitcast.88), calls=%async_computation | async-start | bytes 16777216 | tf_op jit(solution)/shard_map/all_to_all | solution.py:131
  359.1 5.7 copy-start.10
  359.1 298.7 %reduce-scatter.2.cloned.1.call-start = ((), (), s32[]{:S(2)}) async-start(), calls=%async_computation.6 | async-start | bytes 9437184 | tf_op jit(solution)/shard_map/reduce_scatter | solution.py:161
  359.1 3.4 copy-start.3
  362.4 34.6 %collective-permute-start.1 = (bf16[1,176,2,2048]{3,2,1,0:T(2,128)(2,1)S(1)}, bf16[1,176,2,2048]{3,2,1,0:T(2,128)(2,1)}, u32[]{:S(2)}, u32[]{:S(2)}) collective-permute-start(bf16[1,176,2,2048]{3,2,1,0:T(2,128)(2,1)S(1)} %convert_element_type.113), channel_id=1, source_target_pairs={{0,1},{1,0},{2,3},{3,2},{4,5},{5,4},{6,7},{7,6},{8,9},{9,8},{10,11... | collective-permute-start | bytes 4325384 | tf_op jit(solution)/shard_map/ppermute | solution.py:12
  362.6 186.0 %collective-permute-start = (bf16[1,176,2048]{2,1,0:T(8,128)(2,1)S(1)}, bf16[1,176,2048]{2,1,0:T(8,128)(2,1)}, u32[]{:S(2)}, u32[]{:S(2)}) collective-permute-start(bf16[1,176,2048]{2,1,0:T(8,128)(2,1)S(1)} %convert_element_type.112), channel_id=1, source_target_pairs={{0,1},{1,0},{2,3},{3,2},{4,5},{5,4},{6,7},{7,6},{8,9},{9,8},{10,11... | collective-permute-start | bytes 2162696 | tf_op jit(solution)/shard_map/ppermute | solution.py:12
  413.1 135.6 %copy-start.8 = (bf16[1,352,2048]{2,1,0:T(8,128)(2,1)S(1)}, bf16[1,352,2048]{2,1,0:T(8,128)(2,1)}, u32[]{:S(2)}) copy-start(bf16[1,352,2048]{2,1,0:T(8,128)(2,1)} %param.29) | copy-start | bytes 4325380
  657.8 39.3 %all-to-all-start.1 = ((bf16[32,2,32,256]{3,2,1,0:T(8,128)(2,1)}), bf16[32,2,32,256]{3,2,1,0:T(8,128)(2,1)S(1)}, u32[]{:S(2)}, u32[]{:S(2)}) async-start(bf16[32,2,32,256]{3,2,1,0:T(8,128)(2,1)} %reduce-scatter.2.cloned.1.call-done), calls=%async_computation.2 | async-start | bytes 2097152 | tf_op jit(solution)/shard_map/all_to_all | solution.py:162
Sparse Core Ops, SparseCore 0:
  9.1 42.8 all-gather.5
  54.8 82.6 all-gather.7
  140.3 74.7 all-gather.9
  218.0 92.9 all-gather.11
  564.4 93.3 reduce-scatter.1
